TPU v7x, 32 devices: a whole 2x2x4 slice. The times are simulated.
32 devices in a mesh: tm: 8 (over z, core), space: 4 (over y, x).
Axes of the slice: x: 2, y: 2, z: 4, core: 2. Of those that a mesh axis runs over, the one named last changes fastest.
Arguments:
- snapshots: bfloat16 [4096, 12288], P('tm', 'space')
- freq_ids: int32 [64], replicated, may hold values from 0 to 127
Outputs:
- gram: float32 [64, 2, 15, 15], P('tm')
All inputs are finite; a program needn't handle non-finite values.
Results may differ from a plain program's by a relative error of at most 0.00039.
Values may be sent and summed in bfloat16 or wider, within the bound.
No kernel may reach another device: no remote copies, remote signals or barrier semaphores. Data moves between devices by JAX's collectives and lax.ppermute only.
A program may use at most 64 MiB of HBM per device.

v0:
```python
import math
import jax
import jax.numpy as jnp
from jax import lax
from jax.sharding import PartitionSpec as P

NFFT = 512
F = 64


def shifted(block, axis, distance):
    devices = range(lax.axis_size(axis))
    route = [(i - distance, i) for i in devices if i - distance in devices]
    return lax.ppermute(block, axis, route)


def kernel_values(freqs, shifts, window_length):
    phase = freqs * shifts % window_length
    angle = 2.0 * math.pi / window_length * phase.astype(jnp.float32)
    window = 0.5 - 0.5 * jnp.cos(2.0 * math.pi / window_length * shifts.astype(jnp.float32))
    return (window * jnp.cos(angle), -window * jnp.sin(angle))


def local(snapshots, freq_ids):
    hop_len = NFFT // 2
    count_tm = lax.axis_size("tm")
    blocks = 2 * count_tm - 1
    device = lax.axis_index("tm")
    points = snapshots.shape[1]
    shifts = jnp.arange(NFFT, dtype=jnp.int32)
    real_part, imag_part = kernel_values(freq_ids[:, None], shifts[None, :], NFFT)
    table = jnp.stack([real_part, imag_part], axis=1).reshape(2 * F, NFFT).astype(jnp.bfloat16)
    leading = shifted(snapshots[:hop_len], "tm", -1)
    extended = jnp.concatenate([snapshots, leading], axis=0)
    pieces = []
    for slot in range(2):
        block = device * 2 + slot
        segment = extended[hop_len * slot : hop_len * slot + NFFT]
        result = jnp.dot(table, segment, preferred_element_type=jnp.float32)
        pieces.append(jnp.where(block < blocks, result, 0.0))
    owned = jnp.stack(pieces, axis=0).astype(jnp.bfloat16)
    owned = owned.reshape(2, F, 2, points)
    by_freq = lax.all_to_all(owned, "tm", split_axis=1, concat_axis=0, tiled=True)
    slots_all = by_freq.shape[0]
    resident_frequencies = by_freq.shape[1]
    stacked_snapshot_rows = jnp.transpose(by_freq, (1, 2, 0, 3)).reshape(
        resident_frequencies, 2 * slots_all, points
    )
    cross_product_terms = jnp.einsum(
        "tnf,tof->tno",
        stacked_snapshot_rows,
        stacked_snapshot_rows,
        preferred_element_type=jnp.float32,
    )
    gram_real_matrix = (
        cross_product_terms[:, :slots_all, :slots_all]
        + cross_product_terms[:, slots_all:, slots_all:]
    )
    imag_gram = (
        cross_product_terms[:, slots_all:, :slots_all]
        - cross_product_terms[:, :slots_all, slots_all:]
    )
    scale = 1.0 / (NFFT * points * lax.axis_size("space"))
    resident_gram_matrix = (
        jnp.stack([gram_real_matrix, imag_gram], axis=1)[:, :, :blocks, :blocks] * scale
    )
    return lax.psum(resident_gram_matrix, "space")


def solution(mesh):
    return jax.shard_map(
        local,
        mesh=mesh,
        in_specs=(P("tm", "space"), P()),
        out_specs=P("tm", None, None, None),
        check_vma=False,
    )
```

profile of v0, /device:TPU:0, one launch (start us, length us, event | category | flops | bytes accessed | tf_op | source)
XLA Modules:
  0.0 96.8 jit_solution(8468911311742353693)
XLA Ops:
  0.0 0.0 copy-start
  0.0 0.0 copy-start.2
  0.0 2.8 %slice.21 = bf16[256,3072]{1,0:T(8,128)(2,1)} slice(bf16[512,3072]{1,0:T(8,128)(2,1)} %param.2), slice={[0:256], [0:3072]} | slice | bytes 3145728 | tf_op jit(solution)/shard_map/slice | solution.py:33
  2.8 1.3 %collective-permute-start = (bf16[256,3072]{1,0:T(8,128)(2,1)}, bf16[256,3072]{1,0:T(8,128)(2,1)}, u32[]{:S(2)}, u32[]{:S(2)}) collective-permute-start(bf16[256,3072]{1,0:T(8,128)(2,1)} %slice.21), channel_id=1, source_target_pairs={{4,0},{8,4},{12,8},{16,12},{20,16},{24,20},{28,24},{5,1},{9,5},{13... | collective-permute-start | bytes 4718600 | tf_op jit(solution)/shard_map/ppermute | solution.py:14
  4.2 0.0 copy-done.2
  4.2 0.6 multiply_convert_fusion.1
  4.8 0.1 copy.13
  5.0 0.1 convert_element_type.35
  5.0 0.0 copy-done
  5.0 1.5 %fusion = bf16[128,3072]{1,0:T(8,128)(2,1)} fusion(bf16[128,512]{1,0:T(8,128)(2,1)S(1)} %convert_element_type.35, bf16[512,3072]{1,0:T(8,128)(2,1)S(1)} %copy-done, pred[]{:T(512)S(6)} %lt.12), kind=kOutput, calls=%fused_computation.2 | convolution fusion | flops 403439616 | bytes 4063233 | tf_op jit(solution)/shard_map/dot_general | solution.py:39
  6.5 2.8 %stack.25 = bf16[1,64,2,3072]{3,2,1,0:T(2,128)(2,1)} reshape(bf16[128,3072]{1,0:T(8,128)(2,1)} %fusion) | data formatting | bytes 1572864 | tf_op jit(solution)/shard_map/stack | solution.py:41
  9.4 0.0 collective-permute-done
  9.4 2.9 %fusion.1 = bf16[128,3072]{1,0:T(8,128)(2,1)} fusion(bf16[128,512]{1,0:T(8,128)(2,1)S(1)} %convert_element_type.35, bf16[256,3072]{1,0:T(8,128)(2,1)} %collective-permute-done, bf16[512,3072]{1,0:T(8,128)(2,1)S(1)} %copy-done, pred[]{:T(512)S(6)} %lt.14), kind=kOutput, calls=%fused_computation.3 | convolution fusion | flops 409731072 | bytes 5636097 | tf_op jit(solution)/shard_map/dot_general | solution.py:39
  12.3 0.0 copy-start.1
  12.3 2.2 %stack.26 = bf16[1,64,2,3072]{3,2,1,0:T(2,128)(2,1)S(1)} reshape(bf16[128,3072]{1,0:T(8,128)(2,1)} %fusion.1) | data formatting | bytes 1572864 | tf_op jit(solution)/shard_map/stack | solution.py:41
  14.5 0.0 copy-done.1
  14.5 2.1 %pad_maximum_fusion.2 = bf16[2,64,2,3072]{3,2,0,1:T(2,128)(2,1)S(1)} fusion(bf16[1,64,2,3072]{3,2,0,1:T(2,128)(2,1)S(1)} %bitcast.22, bf16[1,64,2,3072]{3,2,0,1:T(2,128)(2,1)S(1)} %bitcast.21), kind=kLoop, calls=%fused_computation.6 | loop fusion | flops 786432 | bytes 3145728 | tf_op jit(solution)/shard_map/stack | solution.py:41
  16.6 58.0 %all_to_all.18 = bf16[2,64,2,3072]{3,2,0,1:T(2,128)(2,1)S(1)} all-to-all(bf16[2,64,2,3072]{3,2,0,1:T(2,128)(2,1)S(1)} %pad_maximum_fusion.2), channel_id=1, replica_groups=mesh['tm'=8,'space'=4] {'tm'}, dimensions={1} | all-to-all | bytes 3145728 | tf_op jit(solution)/shard_map/all_to_all | solution.py:43
  74.6 1.7 %copy.16 = bf16[8,2,8,2,3072]{4,1,0,3,2:T(2,128)(2,1)S(1)} copy(bf16[8,2,8,2,3072]{4,3,1,2,0:T(2,128)(2,1)S(1)} %bitcast.20) | data formatting | bytes 3145728 | tf_op jit(solution)/shard_map/all_to_all | solution.py:43
  76.3 0.6 all_to_all.16
  76.9 0.5 fusion.14
  77.5 0.1 fusion.11
  77.6 18.4 %psum.7 = f32[8,2,15,15]{3,2,0,1:T(8,128)S(1)} all-reduce(f32[8,2,15,15]{3,2,0,1:T(8,128)S(1)} %fusion.6), channel_id=1, replica_groups=mesh['tm'=8,'space'=4] {'space'}, use_global_device_ids=true, to_apply=%region_0.1 | all-reduce | flops 3600 | bytes 28800 | tf_op jit(solution)/shard_map/psum | solution.py:67
  96.0 0.7 copy.17
  (3 shorter events, 0.1 us)
Async XLA Ops:
  0.0 5.0 %copy-start = (bf16[512,3072]{1,0:T(8,128)(2,1)S(1)}, bf16[512,3072]{1,0:T(8,128)(2,1)}, u32[]{:S(2)}) copy-start(bf16[512,3072]{1,0:T(8,128)(2,1)} %param.2) | copy-start | bytes 9437188
  0.0 4.2 %copy-start.2 = (s32[64]{0:T(128)S(1)}, s32[64]{0:T(128)}, u32[]{:S(2)}) copy-start(s32[64]{0:T(128)} %param.3) | copy-start | bytes 772
  2.8 6.5 %collective-permute-start = (bf16[256,3072]{1,0:T(8,128)(2,1)}, bf16[256,3072]{1,0:T(8,128)(2,1)}, u32[]{:S(2)}, u32[]{:S(2)}) collective-permute-start(bf16[256,3072]{1,0:T(8,128)(2,1)} %slice.21), channel_id=1, source_target_pairs={{4,0},{8,4},{12,8},{16,12},{20,16},{24,20},{28,24},{5,1},{9,5},{13... | collective-permute-start | bytes 4718600 | tf_op jit(solution)/shard_map/ppermute | solution.py:14
  12.3 2.2 %copy-start.1 = (bf16[1,64,2,3072]{3,2,1,0:T(2,128)(2,1)S(1)}, bf16[1,64,2,3072]{3,2,1,0:T(2,128)(2,1)}, u32[]{:S(2)}) copy-start(bf16[1,64,2,3072]{3,2,1,0:T(2,128)(2,1)} %stack.25) | copy-start | bytes 2359300
where the time goes:
time: 97 us; the launch traced here: 96.8 us
  blocking collectives  76.4 us (79%)
  local copies, waits for them, and re-layouts  11.2 us (12%)
  matrix products  4.92 us (5%)
  other arithmetic  2.86 us (3%)
  starting transfers between devices  1.28 us (1%)
    all_to_all x1, blocking collectives, local(): lax.all_to_all(owned, 'tm', split_axis=1, concat_axis=0, tiled=True)  58 us
    psum x1, blocking collectives, local(): return lax.psum(resident_gram_matrix, 'space')  18.4 us
    another operation x2, local copies, waits for them, and re-layouts, local(): owned = jnp.stack(pieces, axis=0).astype(jnp.bfloat16)  5.07 us
    dot_general x2, matrix products, local(): result = jnp.dot(table, segment, preferred_element_type=jnp.float32)  4.38 us
    slice x1, local copies, waits for them, and re-layouts, local(): leading = shifted(snapshots[:hop_len], 'tm', -1)  2.83 us
    all_to_all x2, local copies, waits for them, and re-layouts, local(): lax.all_to_all(owned, 'tm', split_axis=1, concat_axis=0, tiled=True)  2.33 us
    another operation x1, other arithmetic, local(): owned = jnp.stack(pieces, axis=0).astype(jnp.bfloat16)  2.07 us
  transfers between devices with their start and end apart: 1, of which 0 were waited for; matrix products, arithmetic and copies ran while one was open for 5% of the time, Pallas kernels for 0%

commit v1 on v0

--- a/solution.py
+++ b/solution.py
@@ -6,6 +6,18 @@
 
 NFFT = 512
 F = 64
+
+
+def split_up(x, dim, count):
+    lengths = x.shape
+    tiles = x.reshape(*lengths[:dim], count, lengths[dim] // count, *lengths[dim + 1 :])
+    return jnp.moveaxis(tiles, dim, 0)
+
+
+def laid_out(tiles, dim):
+    tiles = jnp.moveaxis(tiles, 0, dim)
+    shape = tiles.shape
+    return tiles.reshape(*shape[:dim], shape[dim] * shape[dim + 1], *shape[dim + 2 :])
 
 
 def shifted(block, axis, distance):
@@ -40,7 +52,15 @@
         pieces.append(jnp.where(block < blocks, result, 0.0))
     owned = jnp.stack(pieces, axis=0).astype(jnp.bfloat16)
     owned = owned.reshape(2, F, 2, points)
-    by_freq = lax.all_to_all(owned, "tm", split_axis=1, concat_axis=0, tiled=True)
+    length, position = (lax.axis_size("tm"), lax.axis_index("tm"))
+    tiles = split_up(owned, 1, length)
+    filled = tiles
+    for hop in range(1, length):
+        target, source = ((position + hop) % length, (position - hop) % length)
+        sent = lax.dynamic_index_in_dim(tiles, target, 0)
+        other = lax.ppermute(sent, "tm", [(i_2, (i_2 + hop) % length) for i_2 in range(length)])
+        filled = lax.dynamic_update_slice_in_dim(filled, other, source, axis=0)
+    by_freq = laid_out(filled, 0)
     slots_all = by_freq.shape[0]
     resident_frequencies = by_freq.shape[1]
     stacked_snapshot_rows = jnp.transpose(by_freq, (1, 2, 0, 3)).reshape(

time: 97 us -> 85.5 us (0.88)
  the two profiles are of different devices: /device:TPU:0 before, /device:TPU:8 now
where the time goes in v1:
time: 85.5 us; the launch traced here: 85.3 us
  waiting for transfers between devices  43.6 us (51%)
  blocking collectives  18.8 us (22%)
  starting transfers between devices  9.71 us (11%)
  local copies, waits for them, and re-layouts  7.63 us (9%)
  matrix products  4.48 us (5%)
    ppermute x7, waiting for transfers between devices, local(): lax.ppermute(sent, 'tm', [(i_2, (i_2 + hop) % length) for i_2 in range(le...  28.1 us
    psum x1, blocking collectives, local(): return lax.psum(resident_gram_matrix, 'space')  18.8 us
    ppermute x1, waiting for transfers between devices, shifted(): return lax.ppermute(block, axis, route)  15.5 us
    ppermute x7, starting transfers between devices, local(): lax.ppermute(sent, 'tm', [(i_2, (i_2 + hop) % length) for i_2 in range(le...  7.8 us
    dot_general x2, matrix products, local(): result = jnp.dot(table, segment, preferred_element_type=jnp.float32)  3.95 us
    slice x1, local copies, waits for them, and re-layouts, local(): leading = shifted(snapshots[:hop_len], 'tm', -1)  2.83 us
    another operation x3, local copies, waits for them, and re-layouts, local(): owned = jnp.stack(pieces, axis=0).astype(jnp.bfloat16)  2.6 us
    ppermute x1, starting transfers between devices, shifted(): return lax.ppermute(block, axis, route)  1.91 us
  transfers between devices with their start and end apart: 8, of which 5 were waited for; matrix products, arithmetic and copies ran while one was open for 6% of the time, Pallas kernels for 0%

profile of v1, /device:TPU:8, one launch (start us, length us, event | category | flops | bytes accessed | tf_op | source)
XLA Modules:
  0.0 85.3 jit_solution(16886957333334401100)
XLA Ops:
  0.0 0.0 copy-start
  0.0 0.0 copy-start.1
  0.0 2.8 %slice.21 = bf16[256,3072]{1,0:T(8,128)(2,1)} slice(bf16[512,3072]{1,0:T(8,128)(2,1)} %param.2), slice={[0:256], [0:3072]} | slice | bytes 3145728 | tf_op jit(solution)/shard_map/slice | solution.py:45
  2.8 1.9 %collective-permute-start = (bf16[256,3072]{1,0:T(8,128)(2,1)}, bf16[256,3072]{1,0:T(8,128)(2,1)}, u32[]{:S(2)}, u32[]{:S(2)}) collective-permute-start(bf16[256,3072]{1,0:T(8,128)(2,1)} %slice.21), channel_id=1, source_target_pairs={{4,0},{8,4},{12,8},{16,12},{20,16},{24,20},{28,24},{5,1},{9,5},{13... | collective-permute-start | bytes 4718600 | tf_op jit(solution)/shard_map/ppermute | solution.py:26
  4.9 0.0 copy-done.1
  4.9 0.6 multiply_convert_fusion.1
  5.5 0.1 copy.15
  5.7 0.1 convert_element_type.35
  5.7 0.0 copy-done
  5.7 1.5 %fusion = bf16[128,3072]{1,0:T(8,128)(2,1)} fusion(bf16[128,512]{1,0:T(8,128)(2,1)S(1)} %convert_element_type.35, bf16[512,3072]{1,0:T(8,128)(2,1)S(1)} %copy-done, pred[]{:T(512)S(6)} %lt.113), kind=kOutput, calls=%fused_computation.2 | convolution fusion | flops 403439616 | bytes 4063233 | tf_op jit(solution)/shard_map/dot_general | solution.py:51
  7.2 2.2 %stack.25 = bf16[1,8,8,2,3072]{4,3,2,1,0:T(2,128)(2,1)S(1)} reshape(bf16[128,3072]{1,0:T(8,128)(2,1)} %fusion) | data formatting | bytes 1572864 | tf_op jit(solution)/shard_map/stack | solution.py:53
  9.4 0.1 copy_dynamic-update-slice_fusion.1
  9.6 15.5 %collective-permute-done = bf16[256,3072]{1,0:T(8,128)(2,1)} collective-permute-done((bf16[256,3072]{1,0:T(8,128)(2,1)}, bf16[256,3072]{1,0:T(8,128)(2,1)}, u32[]{:S(2)}, u32[]{:S(2)}) %collective-permute-start) | collective-permute-done | bytes 1572896 | tf_op jit(solution)/shard_map/ppermute | solution.py:26
  25.1 2.5 %fusion.1 = bf16[128,3072]{1,0:T(8,128)(2,1)S(1)} fusion(bf16[128,512]{1,0:T(8,128)(2,1)S(1)} %convert_element_type.35, bf16[256,3072]{1,0:T(8,128)(2,1)} %collective-permute-done, bf16[512,3072]{1,0:T(8,128)(2,1)} %param.2, pred[]{:T(512)S(6)} %lt.115), kind=kOutput, calls=%fused_computation.3 | convolution fusion | flops 409731072 | bytes 5636097 | tf_op jit(solution)/shard_map/dot_general | solution.py:51
  27.6 0.3 stack.26
  27.9 0.1 copy_dynamic-update-slice_fusion
  28.0 0.1 dynamic-slice_bitcast_fusion
  28.1 1.9 %collective-permute-start.1 = (bf16[1,2,8,2,3072]{4,2,3,1,0:T(8,128)(2,1)S(1)}, bf16[1,2,8,2,3072]{4,2,3,1,0:T(8,128)(2,1)S(1)}, u32[]{:S(2)}, u32[]{:S(2)}) collective-permute-start(bf16[1,2,8,2,3072]{4,2,3,1,0:T(8,128)(2,1)S(1)} %get-tuple-element.11), channel_id=1, source_target_pairs={{0,4},{4,8},{8,12},{12,16},{16,20},{20,24},{24,28},{28,0},{1,5},{5... | collective-permute-start | bytes 589832 | tf_op jit(solution)/shard_map/ppermute | solution.py:61
  30.0 1.6 %collective-permute-start.2 = (bf16[1,2,8,2,3072]{4,2,3,1,0:T(8,128)(2,1)S(1)}, bf16[1,2,8,2,3072]{4,2,3,1,0:T(8,128)(2,1)S(1)}, u32[]{:S(2)}, u32[]{:S(2)}) collective-permute-start(bf16[1,2,8,2,3072]{4,2,3,1,0:T(8,128)(2,1)S(1)} %get-tuple-element.10), channel_id=1, source_target_pairs={{0,8},{4,12},{8,16},{12,20},{16,24},{20,28},{24,0},{28,4},{1,9},{5... | collective-permute-start | bytes 589832 | tf_op jit(solution)/shard_map/ppermute | solution.py:61
  31.6 0.0 collective-permute-start.3
  31.6 2.3 %collective-permute-start.4 = (bf16[1,2,8,2,3072]{4,2,3,1,0:T(8,128)(2,1)S(1)}, bf16[1,2,8,2,3072]{4,2,3,1,0:T(8,128)(2,1)S(1)}, u32[]{:S(2)}, u32[]{:S(2)}) collective-permute-start(bf16[1,2,8,2,3072]{4,2,3,1,0:T(8,128)(2,1)S(1)} %get-tuple-element.8), channel_id=1, source_target_pairs={{0,16},{4,20},{8,24},{12,28},{16,0},{20,4},{24,8},{28,12},{1,17},{... | collective-permute-start | bytes 589832 | tf_op jit(solution)/shard_map/ppermute | solution.py:61
  34.0 1.3 %collective-permute-start.5 = (bf16[1,2,8,2,3072]{4,2,3,1,0:T(8,128)(2,1)S(1)}, bf16[1,2,8,2,3072]{4,2,3,1,0:T(8,128)(2,1)S(1)}, u32[]{:S(2)}, u32[]{:S(2)}) collective-permute-start(bf16[1,2,8,2,3072]{4,2,3,1,0:T(8,128)(2,1)S(1)} %get-tuple-element.7), channel_id=1, source_target_pairs={{0,20},{4,24},{8,28},{12,0},{16,4},{20,8},{24,12},{28,16},{1,21},{... | collective-permute-start | bytes 589832 | tf_op jit(solution)/shard_map/ppermute | solution.py:61
  35.2 0.0 collective-permute-done.1
  35.2 0.2 collective-permute-start.6
  35.5 2.3 %collective-permute-done.2 = bf16[1,2,8,2,3072]{4,2,3,1,0:T(8,128)(2,1)S(1)} collective-permute-done((bf16[1,2,8,2,3072]{4,2,3,1,0:T(8,128)(2,1)S(1)}, bf16[1,2,8,2,3072]{4,2,3,1,0:T(8,128)(2,1)S(1)}, u32[]{:S(2)}, u32[]{:S(2)}) %collective-permute-start.2) | collective-permute-done | bytes 196640 | tf_op jit(solution)/shard_map/ppermute | solution.py:61
  37.8 0.5 collective-permute-start.7
  38.3 19.6 %collective-permute-done.3 = bf16[1,2,8,2,3072]{4,2,3,1,0:T(8,128)(2,1)S(1)} collective-permute-done((bf16[1,2,8,2,3072]{4,2,3,1,0:T(8,128)(2,1)S(1)}, bf16[1,2,8,2,3072]{4,2,3,1,0:T(8,128)(2,1)S(1)}, u32[]{:S(2)}, u32[]{:S(2)}) %collective-permute-start.3) | collective-permute-done | bytes 196640 | tf_op jit(solution)/shard_map/ppermute | solution.py:61
  58.0 4.0 %collective-permute-done.4 = bf16[1,2,8,2,3072]{4,2,3,1,0:T(8,128)(2,1)S(1)} collective-permute-done((bf16[1,2,8,2,3072]{4,2,3,1,0:T(8,128)(2,1)S(1)}, bf16[1,2,8,2,3072]{4,2,3,1,0:T(8,128)(2,1)S(1)}, u32[]{:S(2)}, u32[]{:S(2)}) %collective-permute-start.4) | collective-permute-done | bytes 196640 | tf_op jit(solution)/shard_map/ppermute | solution.py:61
  62.1 2.1 %collective-permute-done.5 = bf16[1,2,8,2,3072]{4,2,3,1,0:T(8,128)(2,1)S(1)} collective-permute-done((bf16[1,2,8,2,3072]{4,2,3,1,0:T(8,128)(2,1)S(1)}, bf16[1,2,8,2,3072]{4,2,3,1,0:T(8,128)(2,1)S(1)}, u32[]{:S(2)}, u32[]{:S(2)}) %collective-permute-start.5) | collective-permute-done | bytes 196640 | tf_op jit(solution)/shard_map/ppermute | solution.py:61
  64.2 0.0 collective-permute-done.6
  64.2 0.0 collective-permute-done.7
  64.2 0.9 %copy.18 = bf16[8,2,16,3072]{3,2,1,0:T(8,128)(2,1)S(1)} copy(bf16[8,2,16,3072]{3,0,1,2:T(8,128)(2,1)S(1)} %bitcast.30) | data formatting | bytes 3145728 | tf_op jit(solution)/shard_map/transpose | solution.py:66
  65.1 0.5 fusion.14
  65.7 0.1 fusion.11
  65.8 18.8 %psum.7 = f32[8,2,15,15]{3,2,0,1:T(8,128)S(1)} all-reduce(f32[8,2,15,15]{3,2,0,1:T(8,128)S(1)} %fusion.6), channel_id=1, replica_groups=mesh['tm'=8,'space'=4] {'space'}, use_global_device_ids=true, to_apply=%region_0.1 | all-reduce | flops 3600 | bytes 28800 | tf_op jit(solution)/shard_map/psum | solution.py:87
  84.6 0.7 copy.19
  (10 shorter events, 0.2 us)
Async XLA Ops:
  0.0 5.7 %copy-start = (bf16[512,3072]{1,0:T(8,128)(2,1)S(1)}, bf16[512,3072]{1,0:T(8,128)(2,1)}, u32[]{:S(2)}) copy-start(bf16[512,3072]{1,0:T(8,128)(2,1)} %param.2) | copy-start | bytes 9437188
  0.0 4.9 %copy-start.1 = (s32[64]{0:T(128)S(1)}, s32[64]{0:T(128)}, u32[]{:S(2)}) copy-start(s32[64]{0:T(128)} %param.3) | copy-start | bytes 772
  2.8 22.3 %collective-permute-start = (bf16[256,3072]{1,0:T(8,128)(2,1)}, bf16[256,3072]{1,0:T(8,128)(2,1)}, u32[]{:S(2)}, u32[]{:S(2)}) collective-permute-start(bf16[256,3072]{1,0:T(8,128)(2,1)} %slice.21), channel_id=1, source_target_pairs={{4,0},{8,4},{12,8},{16,12},{20,16},{24,20},{28,24},{5,1},{9,5},{13... | collective-permute-start | bytes 4718600 | tf_op jit(solution)/shard_map/ppermute | solution.py:26
  28.1 7.1 %collective-permute-start.1 = (bf16[1,2,8,2,3072]{4,2,3,1,0:T(8,128)(2,1)S(1)}, bf16[1,2,8,2,3072]{4,2,3,1,0:T(8,128)(2,1)S(1)}, u32[]{:S(2)}, u32[]{:S(2)}) collective-permute-start(bf16[1,2,8,2,3072]{4,2,3,1,0:T(8,128)(2,1)S(1)} %get-tuple-element.11), channel_id=1, source_target_pairs={{0,4},{4,8},{8,12},{12,16},{16,20},{20,24},{24,28},{28,0},{1,5},{5... | collective-permute-start | bytes 589832 | tf_op jit(solution)/shard_map/ppermute | solution.py:61
  30.0 7.8 %collective-permute-start.2 = (bf16[1,2,8,2,3072]{4,2,3,1,0:T(8,128)(2,1)S(1)}, bf16[1,2,8,2,3072]{4,2,3,1,0:T(8,128)(2,1)S(1)}, u32[]{:S(2)}, u32[]{:S(2)}) collective-permute-start(bf16[1,2,8,2,3072]{4,2,3,1,0:T(8,128)(2,1)S(1)} %get-tuple-element.10), channel_id=1, source_target_pairs={{0,8},{4,12},{8,16},{12,20},{16,24},{20,28},{24,0},{28,4},{1,9},{5... | collective-permute-start | bytes 589832 | tf_op jit(solution)/shard_map/ppermute | solution.py:61
  31.6 26.4 %collective-permute-start.3 = (bf16[1,2,8,2,3072]{4,2,3,1,0:T(8,128)(2,1)S(1)}, bf16[1,2,8,2,3072]{4,2,3,1,0:T(8,128)(2,1)S(1)}, u32[]{:S(2)}, u32[]{:S(2)}) collective-permute-start(bf16[1,2,8,2,3072]{4,2,3,1,0:T(8,128)(2,1)S(1)} %get-tuple-element.9), channel_id=1, source_target_pairs={{0,12},{4,16},{8,20},{12,24},{16,28},{20,0},{24,4},{28,8},{1,13},{... | collective-permute-start | bytes 589832 | tf_op jit(solution)/shard_map/ppermute | solution.py:61
  31.6 30.4 %collective-permute-start.4 = (bf16[1,2,8,2,3072]{4,2,3,1,0:T(8,128)(2,1)S(1)}, bf16[1,2,8,2,3072]{4,2,3,1,0:T(8,128)(2,1)S(1)}, u32[]{:S(2)}, u32[]{:S(2)}) collective-permute-start(bf16[1,2,8,2,3072]{4,2,3,1,0:T(8,128)(2,1)S(1)} %get-tuple-element.8), channel_id=1, source_target_pairs={{0,16},{4,20},{8,24},{12,28},{16,0},{20,4},{24,8},{28,12},{1,17},{... | collective-permute-start | bytes 589832 | tf_op jit(solution)/shard_map/ppermute | solution.py:61
  34.0 30.2 %collective-permute-start.5 = (bf16[1,2,8,2,3072]{4,2,3,1,0:T(8,128)(2,1)S(1)}, bf16[1,2,8,2,3072]{4,2,3,1,0:T(8,128)(2,1)S(1)}, u32[]{:S(2)}, u32[]{:S(2)}) collective-permute-start(bf16[1,2,8,2,3072]{4,2,3,1,0:T(8,128)(2,1)S(1)} %get-tuple-element.7), channel_id=1, source_target_pairs={{0,20},{4,24},{8,28},{12,0},{16,4},{20,8},{24,12},{28,16},{1,21},{... | collective-permute-start | bytes 589832 | tf_op jit(solution)/shard_map/ppermute | solution.py:61
  35.2 28.9 %collective-permute-start.6 = (bf16[1,2,8,2,3072]{4,2,3,1,0:T(8,128)(2,1)S(1)}, bf16[1,2,8,2,3072]{4,2,3,1,0:T(8,128)(2,1)S(1)}, u32[]{:S(2)}, u32[]{:S(2)}) collective-permute-start(bf16[1,2,8,2,3072]{4,2,3,1,0:T(8,128)(2,1)S(1)} %get-tuple-element.6), channel_id=1, source_target_pairs={{0,24},{4,28},{8,0},{12,4},{16,8},{20,12},{24,16},{28,20},{1,25},{... | collective-permute-start | bytes 589832 | tf_op jit(solution)/shard_map/ppermute | solution.py:61
  37.8 26.4 %collective-permute-start.7 = (bf16[1,2,8,2,3072]{4,2,3,1,0:T(8,128)(2,1)S(1)}, bf16[1,2,8,2,3072]{4,2,3,1,0:T(8,128)(2,1)S(1)}, u32[]{:S(2)}, u32[]{:S(2)}) collective-permute-start(bf16[1,2,8,2,3072]{4,2,3,1,0:T(8,128)(2,1)S(1)} %get-tuple-element.5), channel_id=1, source_target_pairs={{0,28},{4,0},{8,4},{12,8},{16,12},{20,16},{24,20},{28,24},{1,29},{... | collective-permute-start | bytes 589832 | tf_op jit(solution)/shard_map/ppermute | solution.py:61
